TPU v7x, 256 devices: a whole 4x4x8 slice. The times are simulated.
256 devices in a mesh: row: 8 (over z), col: 16 (over x_hi, y, core), rep: 2 (over x_lo).
Axes of the slice: x: 4 (x_hi: 2, x_lo: 2; x = x_hi * 2 + x_lo), y: 4, z: 8, core: 2. Of those that a mesh axis runs over, the one named last changes fastest.
Arguments:
- descriptors: float32 [2048, 256], P('rep', 'col'), may hold values from -6 to 6
- landmarks: float32 [12288, 256], P('row', 'col'), may hold values from -6 to 6
- whitening: float32 [12288, 12288], P('row', 'col'), may hold values from -1 to 1
- assign: int32 [2048], replicated, may hold values from 0 to 4095
Outputs:
- cluster_sums: float32 [4096, 12288], P(('row', 'rep'), 'col')
All inputs are finite; a program needn't handle non-finite values.
Results may differ from a plain program's by a relative error of at most 0.00016.
Values sent between devices are 32-bit elements; how exact they have to be, the bound alone decides.
A program may use at most 64 MiB of HBM per device.

v0:
```python
import jax
import jax.numpy as jnp
from jax import lax
from jax.sharding import PartitionSpec as P

SPREAD = 51
CLUSTERS = 4096
highest = lax.Precision.HIGHEST


def kernel_tile(points, centres):
    row_square = jnp.sum(points * points, axis=1)
    centre_square = jnp.sum(centres * centres, axis=1)
    inner = jnp.dot(points, centres.T, precision=highest, preferred_element_type=jnp.float32)
    distance = row_square[:, None] + centre_square[None, :] - 2.0 * inner
    return jnp.exp(-distance / (2.0 * SPREAD))


def per_device(descriptors, landmarks, whitening, assign):
    part_rows = descriptors.shape[0]
    rep_position = lax.axis_index("rep")
    full_points, full_centres = (
        lax.all_gather(descriptors, "col", axis=1, tiled=True),
        lax.all_gather(landmarks, "col", axis=1, tiled=True),
    )
    kernel = kernel_tile(full_points, full_centres)
    whitened = jnp.dot(kernel, whitening, precision=highest, preferred_element_type=jnp.float32)
    owned_count = CLUSTERS // (lax.axis_size("row") * lax.axis_size("rep"))
    local_assign = lax.dynamic_slice_in_dim(assign, rep_position * part_rows, part_rows)
    labels = jnp.arange(owned_count * lax.axis_size(("row", "rep")), dtype=jnp.int32)
    onehot = (labels[:, None] == local_assign[None, :]).astype(jnp.float32)
    return lax.psum_scatter(
        jnp.dot(onehot, whitened, precision=highest, preferred_element_type=jnp.float32),
        ("row", "rep"),
        scatter_dimension=0,
        tiled=True,
    )


def solution(mesh):
    placed = (P("rep", "col"), P("row", "col"), P("row", "col"), P())
    return jax.shard_map(
        per_device, mesh=mesh, in_specs=placed, out_specs=P(("row", "rep"), "col"), check_vma=False
    )
```

profile of v0, /device:TPU:1, one launch (start us, length us, event | category | flops | bytes accessed | tf_op | source)
XLA Modules:
  0.0 440.5 jit_solution(17535972358049037863)
XLA Ops:
  6.5 0.0 all-gather.3.cloned.1.call-start
  6.5 0.7 all-gather.3.cloned.1.call-update
  7.3 0.0 all-gather.5.cloned.1.call-start
  7.3 0.7 all-gather.5.cloned.1.call-update
  8.0 0.0 reduce-scatter.2.cloned.1.call-start
  8.1 56.2 %all-gather.3.cloned.1.call-done = f32[1024,256]{0,1:T(8,128)} async-done(((f32[1024,16]{0,1:T(8,128)}), f32[1024,256]{0,1:T(8,128)}) %all-gather.3.cloned.1.call-update) | async-done | bytes 1048592 | tf_op jit(solution)/shard_map/all_gather | solution.py:23
  64.2 1.3 multiply_reduce_fusion.1
  65.6 51.5 %all-gather.5.cloned.1.call-done = f32[1536,256]{0,1:T(8,128)} async-done(((f32[1536,16]{0,1:T(8,128)}), f32[1536,256]{0,1:T(8,128)}) %all-gather.5.cloned.1.call-update) | async-done | bytes 1572880 | tf_op jit(solution)/shard_map/all_gather | solution.py:24
  117.1 0.0 slice-start
  117.1 1.7 multiply_reduce_fusion
  118.8 0.0 slice-start.1
  118.8 7.3 %fusion.15 = f32[1024,1536]{1,0:T(8,128)S(1)} fusion(f32[1024,256]{0,1:T(8,128)} %all-gather.3.cloned.1.call-done, f32[1536,256]{0,1:T(8,128)} %all-gather.5.cloned.1.call-done), kind=kOutput, calls=%fused_computation.18 | convolution fusion | flops 4831838208 | bytes 8912896 | tf_op jit(solution)/shard_map/dot_general | solution.py:14
  126.1 0.0 slice-done
  126.2 0.0 slice-done.1
  126.2 0.0 dynamic-slice-start
  126.2 16.3 %fusion.2 = f32[1024,768]{1,0:T(8,128)S(1)} fusion(f32[1536,768]{1,0:T(8,128)S(1)} %bitcast.5, f32[1024,1536]{1,0:T(8,128)S(1)} %fusion.15, f32[1536]{0:T(1024)S(1)} %multiply_reduce_fusion, f32[1024]{0:T(1024)S(1)} %multiply_reduce_fusion.1), kind=kOutput, calls=%fused_computation.3 | convolution fusion | flops 14503378944 | bytes 14166016 | tf_op jit(solution)/shard_map/dot_general | solution.py:27
  142.5 0.0 dynamic-slice-done
  142.5 25.8 %fusion = f32[4096,768]{1,0:T(8,128)} fusion(f32[1024,768]{1,0:T(8,128)S(1)} %fusion.2, s32[1024]{0:T(1024)S(1)} %dynamic-slice-done), kind=kOutput, calls=%fused_computation.1 | convolution fusion | flops 38658899968 | bytes 15732736 | tf_op jit(solution)/shard_map/dot_general | solution.py:33
  168.3 0.0 reduce-scatter.2.cloned.1.call-update
  168.3 265.7 %reduce-scatter.2.cloned.1.call-done = f32[256,768]{1,0:T(8,128)} async-done(((f32[4096,768]{1,0:T(8,128)}), f32[256,768]{1,0:T(8,128)}) %reduce-scatter.2.cloned.1.call-update) | async-done | bytes 786448 | tf_op jit(solution)/shard_map/reduce_scatter | solution.py:32
  (1 shorter events, 0.0 us)
Async XLA Ops:
  6.5 57.7 %all-gather.3.cloned.1.call-start = ((), (), s32[]{:S(2)}) async-start(), calls=%async_computation.1 | async-start | bytes 1114112 | tf_op jit(solution)/shard_map/all_gather | solution.py:23
  7.3 109.8 %all-gather.5.cloned.1.call-start = ((), (), s32[]{:S(2)}) async-start(), calls=%async_computation.2 | async-start | bytes 1671168 | tf_op jit(solution)/shard_map/all_gather | solution.py:24
  8.0 426.0 %reduce-scatter.2.cloned.1.call-start = ((), (), s32[]{:S(2)}) async-start(), calls=%async_computation.3 | async-start | bytes 13369344 | tf_op jit(solution)/shard_map/reduce_scatter | solution.py:32
  117.1 9.0 %slice-start = ((s8[4718592]{0:T(1024)(128)(4,1)}), s8[4194304]{0:T(1024)(128)(4,1)S(1)}, s32[]{:S(2)}) async-start(s8[4718592]{0:T(1024)(128)(4,1)} %bitcast.4), calls=%async_computation.5 | async-start | bytes 8388608
  118.8 7.4 %slice-start.1 = ((s8[4718592]{0:T(1024)(128)(4,1)}), s8[524288]{0:T(1024)(128)(4,1)S(1)}, s32[]{:S(2)}) async-start(s8[4718592]{0:T(1024)(128)(4,1)} %bitcast.4), calls=%async_computation.6 | async-start | bytes 1048576
  126.2 16.3 %dynamic-slice-start = ((s32[2048]{0:T(1024)}, s32[]{:T(128)}), s32[1024]{0:T(1024)S(1)}, s32[]{:S(2)}) async-start(s32[2048]{0:T(1024)} %param.7, s32[]{:T(128)} %select_n.3), calls=%async_computation.4 | async-start | bytes 8704 | tf_op jit(solution)/shard_map/dynamic_slice | solution.py:29
Sparse Core Ops, SparseCore 0:
  10.1 54.0 all-gather.2
  67.0 50.0 all-gather.4
  168.4 265.5 reduce-scatter.1
where the time goes:
time: 441 us
  waiting for transfers between devices  375 us (85%)
  matrix products  49.4 us (11%)
  between operations  13.2 us (3%)
    reduce_scatter x1, waiting for transfers between devices, per_device(): lax.psum_scatter(jnp.dot(onehot, whitened, precision=highest, preferred_e...  266 us
    all_gather x1, waiting for transfers between devices, per_device(): lax.all_gather(descriptors, 'col', axis=1, tiled=True)  56.2 us
    all_gather x1, waiting for transfers between devices, per_device(): lax.all_gather(landmarks, 'col', axis=1, tiled=True)  51.5 us
    dot_general x1, matrix products, per_device(): jnp.dot(onehot, whitened, precision=highest, preferred_element_type=jnp.f...  25.8 us
    dot_general x1, matrix products, per_device(): jnp.dot(kernel, whitening, precision=highest, preferred_element_type=jnp....  16.3 us
  transfers between devices with their start and end apart: 3, of which 3 were waited for; matrix products, arithmetic and copies ran while one was open for 0% of the time, Pallas kernels for 0%

commit v1 on v0

--- a/solution.py
+++ b/solution.py
@@ -2,10 +2,18 @@
 import jax.numpy as jnp
 from jax import lax
 from jax.sharding import PartitionSpec as P
+from jax.lax import all_to_all, axis_size
 
 SPREAD = 51
 CLUSTERS = 4096
 highest = lax.Precision.HIGHEST
+
+
+def _compute_orders(view):
+    v1 = jnp.concatenate(
+        all_to_all(jnp.stack(axis_size("col") * [view]), "col", split_axis=0, concat_axis=0), axis=1
+    )
+    return v1
 
 
 def kernel_tile(points, centres):
@@ -20,7 +28,7 @@
     part_rows = descriptors.shape[0]
     rep_position = lax.axis_index("rep")
     full_points, full_centres = (
-        lax.all_gather(descriptors, "col", axis=1, tiled=True),
+        _compute_orders(descriptors),
         lax.all_gather(landmarks, "col", axis=1, tiled=True),
     )
     kernel = kernel_tile(full_points, full_centres)

time: 441 us -> 391 us (0.89)
  waiting for transfers between devices: 375 us -> 316 us
  starting transfers between devices: 0.08 us -> 8.49 us
    all_gather x1 -> x0, waiting for transfers between devices: 56.2 us -> none  [per_device(): lax.all_gather(descriptors, 'col', axis=1, tiled=True)]
    all_gather x1, waiting for transfers between devices: 51.5 us -> 31.5 us  [per_device(): lax.all_gather(landmarks, 'col', axis=1, tiled=True)]
    all_to_all x0 -> x1, waiting for transfers between devices: none -> 18.2 us  [_compute_orders(): all_to_all(jnp.stack(axis_size('col') * [view]), 'col', split_axis=0, con...]
    all_to_all x0 -> x1, starting transfers between devices: none -> 8.45 us  [_compute_orders(): all_to_all(jnp.stack(axis_size('col') * [view]), 'col', split_axis=0, con...]
  transfers between devices with their start and end apart: 3 -> 3, of which waited for: 3 -> 3; matrix products, arithmetic and copies ran while one was open for 0% -> 1% of each run, Pallas kernels for 0% -> 0%
where the time goes in v1:
time: 391 us
  waiting for transfers between devices  316 us (81%)
  matrix products  49.1 us (13%)
  between operations  13.5 us (3%)
  starting transfers between devices  8.49 us (2%)
    reduce_scatter x1, waiting for transfers between devices, per_device(): lax.psum_scatter(jnp.dot(onehot, whitened, precision=highest, preferred_e...  266 us
    all_gather x1, waiting for transfers between devices, per_device(): lax.all_gather(landmarks, 'col', axis=1, tiled=True)  31.5 us
    dot_general x1, matrix products, per_device(): jnp.dot(onehot, whitened, precision=highest, preferred_element_type=jnp.f...  25.7 us
    all_to_all x1, waiting for transfers between devices, _compute_orders(): all_to_all(jnp.stack(axis_size('col') * [view]), 'col', split_axis=0, con...  18.2 us
    dot_general x1, matrix products, per_device(): jnp.dot(kernel, whitening, precision=highest, preferred_element_type=jnp....  16.3 us
    all_to_all x1, starting transfers between devices, _compute_orders(): all_to_all(jnp.stack(axis_size('col') * [view]), 'col', split_axis=0, con...  8.45 us
  transfers between devices with their start and end apart: 3, of which 3 were waited for; matrix products, arithmetic and copies ran while one was open for 1% of the time, Pallas kernels for 0%

profile of v1, /device:TPU:1, one launch (start us, length us, event | category | flops | bytes accessed | tf_op | source)
XLA Modules:
  0.0 390.9 jit_solution(14331177284963219820)
XLA Ops:
  6.5 0.0 all-gather.2.cloned.1.call-start
  6.5 0.7 all-gather.2.cloned.1.call-update
  7.3 1.9 stack.2
  9.2 8.4 %all-to-all-start = ((f32[16,1024,16]{1,2,0:T(8,128)}), f32[16,1024,16]{1,2,0:T(8,128)S(1)}, u32[]{:S(2)}, u32[]{:S(2)}) async-start(f32[16,1024,16]{1,2,0:T(8,128)} %stack.2), calls=%async_computation | async-start | bytes 2097152 | tf_op jit(solution)/shard_map/all_to_all | solution.py:14
  17.6 0.0 reduce-scatter.2.cloned.1.call-start
  17.7 18.2 %all-to-all-done = f32[16,1024,16]{1,2,0:T(8,128)S(1)} async-done(((f32[16,1024,16]{1,2,0:T(8,128)}), f32[16,1024,16]{1,2,0:T(8,128)S(1)}, u32[]{:S(2)}, u32[]{:S(2)}) %all-to-all-start) | async-done | bytes 1048608 | tf_op jit(solution)/shard_map/all_to_all | solution.py:14
  35.9 0.1 fusion.13
  36.0 31.5 %all-gather.2.cloned.1.call-done = f32[1536,256]{0,1:T(8,128)} async-done(((f32[1536,16]{0,1:T(8,128)}), f32[1536,256]{0,1:T(8,128)}) %all-gather.2.cloned.1.call-update) | async-done | bytes 1572880 | tf_op jit(solution)/shard_map/all_gather | solution.py:32
  67.5 0.0 slice-start
  67.5 1.7 multiply_reduce_fusion
  69.2 0.0 slice-start.1
  69.2 7.0 %fusion.16 = f32[1024,1536]{1,0:T(8,128)S(1)} fusion(f32[1024,256]{0,1:T(8,128)S(1)} %bitcast.10, f32[1536,256]{0,1:T(8,128)} %all-gather.2.cloned.1.call-done), kind=kOutput, calls=%fused_computation.19 | convolution fusion | flops 4831838208 | bytes 8912896 | tf_op jit(solution)/shard_map/dot_general | solution.py:22
  76.2 0.0 slice-done
  76.2 0.0 slice-done.1
  76.2 0.0 dynamic-slice-start
  76.2 16.3 %fusion.2 = f32[1024,768]{1,0:T(8,128)S(1)} fusion(f32[1536,768]{1,0:T(8,128)S(1)} %bitcast.12, f32[1024,1536]{1,0:T(8,128)S(1)} %fusion.16, f32[1536]{0:T(1024)S(1)} %multiply_reduce_fusion, f32[1024]{0:T(1024)S(1)} %fusion.13), kind=kOutput, calls=%fused_computation.3 | convolution fusion | flops 14503378944 | bytes 14166016 | tf_op jit(solution)/shard_map/dot_general | solution.py:35
  92.6 0.0 dynamic-slice-done
  92.6 25.7 %fusion = f32[4096,768]{1,0:T(8,128)} fusion(f32[1024,768]{1,0:T(8,128)S(1)} %fusion.2, s32[1024]{0:T(1024)S(1)} %dynamic-slice-done), kind=kOutput, calls=%fused_computation.1 | convolution fusion | flops 38658899968 | bytes 15732736 | tf_op jit(solution)/shard_map/dot_general | solution.py:41
  118.3 0.0 reduce-scatter.2.cloned.1.call-update
  118.3 265.7 %reduce-scatter.2.cloned.1.call-done = f32[256,768]{1,0:T(8,128)} async-done(((f32[4096,768]{1,0:T(8,128)}), f32[256,768]{1,0:T(8,128)}) %reduce-scatter.2.cloned.1.call-update) | async-done | bytes 786448 | tf_op jit(solution)/shard_map/reduce_scatter | solution.py:40
  (1 shorter events, 0.0 us)
Async XLA Ops:
  6.5 61.0 %all-gather.2.cloned.1.call-start = ((), (), s32[]{:S(2)}) async-start(), calls=%async_computation.2 | async-start | bytes 1671168 | tf_op jit(solution)/shard_map/all_gather | solution.py:32
  9.2 26.7 %all-to-all-start = ((f32[16,1024,16]{1,2,0:T(8,128)}), f32[16,1024,16]{1,2,0:T(8,128)S(1)}, u32[]{:S(2)}, u32[]{:S(2)}) async-start(f32[16,1024,16]{1,2,0:T(8,128)} %stack.2), calls=%async_computation | async-start | bytes 2097152 | tf_op jit(solution)/shard_map/all_to_all | solution.py:14
  17.6 366.4 %reduce-scatter.2.cloned.1.call-start = ((), (), s32[]{:S(2)}) async-start(), calls=%async_computation.3 | async-start | bytes 13369344 | tf_op jit(solution)/shard_map/reduce_scatter | solution.py:40
  67.5 8.7 %slice-start = ((s8[4718592]{0:T(1024)(128)(4,1)}), s8[4194304]{0:T(1024)(128)(4,1)S(1)}, s32[]{:S(2)}) async-start(s8[4718592]{0:T(1024)(128)(4,1)} %bitcast.11), calls=%async_computation.5 | async-start | bytes 8388608
  69.2 7.0 %slice-start.1 = ((s8[4718592]{0:T(1024)(128)(4,1)}), s8[524288]{0:T(1024)(128)(4,1)S(1)}, s32[]{:S(2)}) async-start(s8[4718592]{0:T(1024)(128)(4,1)} %bitcast.11), calls=%async_computation.6 | async-start | bytes 1048576
  76.2 16.3 %dynamic-slice-start = ((s32[2048]{0:T(1024)}, s32[]{:T(128)}), s32[1024]{0:T(1024)S(1)}, s32[]{:S(2)}) async-start(s32[2048]{0:T(1024)} %param.7, s32[]{:T(128)} %select_n.3), calls=%async_computation.4 | async-start | bytes 8704 | tf_op jit(solution)/shard_map/dynamic_slice | solution.py:37
Sparse Core Ops, SparseCore 0:
  10.1 57.3 all-gather.1
  118.5 265.5 reduce-scatter.1
